TPU v7x, 32 devices: a whole 2x2x4 slice. The times are simulated.
32 devices in a mesh: region: 8 (over z, core), state: 4 (over y, x).
Axes of the slice: x: 2, y: 2, z: 4, core: 2. Of those that a mesh axis runs over, the one named last changes fastest.
Arguments:
- state_anom: float32 [8, 16, 256, 512], P('region', 'state'), may hold values from -6 to 6
- obs_anom: float32 [8, 256, 512], P('region', 'state'), may hold values from -6 to 6
- obs_weight: float32 [8, 256, 512], P('region', 'state'), may hold values from -6 to 6
- obs_cell: int32 [8, 256], P('region', 'state'), may hold values from 0 to 255, as said below
- sector_of: int32 [8], replicated, may hold values from 0 to 7, as said below
Outputs:
- increment: float32 [8, 16, 256, 512], P('region', 'state')
Inputs may be any that keep to these rules, and one draw needn't show every extreme that they name: `obs_cell`: each entry is lon * 8 + lat with lon in 0..31 and lat in 0..7. Within each aligned block of 64 entries along the observation dimension the entries do not decrease; in each such block between 8 and 16 entries have lon < 8, and between 8 and 16 have lon >= 24; the bound 16 is reached on both sides in every draw. `sector_of`: A permutation: every region holds a different sector.
All inputs are finite; a program needn't handle non-finite values.
Results may differ from a plain program's by a relative error of at most 0.0003.
Values sent between devices are 32-bit elements; how exact they have to be, the bound alone decides.
No kernel may reach another device: no remote copies, remote signals or barrier semaphores. Data moves between devices by JAX's collectives and lax.ppermute only.
A program may use at most 64 MiB of HBM per device.

v0:
```python
import functools

import jax
import jax.numpy as jnp
from jax import lax
from jax.experimental import pallas as pl
from jax.experimental.pallas import tpu as pltpu
from jax.sharding import PartitionSpec as P


SECT_W = 32
LAT = 8
HALF = 4
CAP = 16
EDGE = 2 * HALF * LAT
SUB = 8
LANES = 128
VMEM = pl.BlockSpec(memory_space=pltpu.VMEM)
SMEM = pl.BlockSpec(memory_space=pltpu.SMEM)
HBM = pl.BlockSpec(memory_space=pltpu.HBM)


def limit(mib):
    return pltpu.CompilerParams(vmem_limit_bytes=mib << 20)


def in_hbm(*values):
    return [pltpu.with_memory_space_constraint(value, pltpu.HBM) for value in values]


def target(index, step, size):
    return index ^ step if size & (size - 1) == 0 else (index + step) % size


def exchange(value, axis, step):
    size = lax.axis_size(axis)
    return lax.ppermute(value, axis, [(i, target(i, step, size)) for i in range(size)])


def gather(value, axis):
    size = lax.axis_size(axis)
    steps = (2, 1) if size == 4 else range(size - 1, 0, -1)
    got = {step: exchange(value, axis, step) for step in steps}
    if size == 4:
        got[3] = [exchange(got[1][0], axis, 2), exchange(got[2][1], axis, 1)]
    return [(half[0], half[1]) if isinstance(half, list) else half for half in [value] + [got[k] for k in range(1, size)]]


def gaspari(scaled):
    inside = scaled * scaled * (scaled * (scaled * (0.5 - 0.25 * scaled) + 0.625) - 5.0 / 3.0) + 1.0
    floored = jnp.maximum(scaled, 1.0)
    outside = (
        scaled * (scaled * (scaled * (scaled * (scaled / 12.0 - 0.5) + 0.625) + 5.0 / 3.0) - 5.0)
        + 4.0
        - 2.0 / (3.0 * floored)
    )
    return jnp.where(scaled <= 1.0, inside, jnp.where(scaled < 2.0, outside, 0.0))


def taper(first_col, rows, cells, lon_shift):
    cols = first_col + lax.broadcasted_iota(jnp.int32, (rows, cells.shape[1]), 0)
    obs = cells.astype(jnp.int32)
    lon_gap = cols // LAT - (obs // LAT + lon_shift)
    lat_gap = cols % LAT - obs % LAT
    scaled = jnp.sqrt((lon_gap * lon_gap + lat_gap * lat_gap).astype(jnp.float32)) / HALF
    return gaspari(scaled)


def split(value):
    high = value.astype(jnp.bfloat16)
    return high, (value - high.astype(jnp.float32)).astype(jnp.bfloat16)


def product(left, right, dims):
    dot = functools.partial(lax.dot_general, dimension_numbers=(dims, ((), ())), preferred_element_type=jnp.float32)
    return dot(left[0], right[0]) + (dot(left[0], right[1]) + dot(left[1], right[0]))


NT = ((1,), (1,))
NN = ((1,), (0,))


def folded(rows):
    return jnp.concatenate([rows[i : i + SUB] for i in range(0, rows.shape[0], SUB)], axis=1)


def unfolded(tiles, members):
    return jnp.concatenate([tiles[:, i : i + members] for i in range(0, tiles.shape[1], members)], axis=0)


def pack_kernel(sector_hbm, anom_hbm, weight_hbm, cell_hbm, own_ref, *refs):
    side_ref, cross_ref, *near_refs, sector_ref, anom_ref, weight_ref, cell_ref, sems = refs
    count, members = weight_ref.shape
    loads = [
        pltpu.make_async_copy(cell_hbm, cell_ref, sems.at[0]),
        pltpu.make_async_copy(sector_hbm, sector_ref, sems.at[1]),
        pltpu.make_async_copy(weight_hbm.at[0], weight_ref, sems.at[2]),
        pltpu.make_async_copy(anom_hbm.at[0], anom_ref, sems.at[3]),
    ]
    for load in loads:
        load.start()
    regions = lax.axis_size("region")
    half_way = regions // 2
    me = lax.axis_index("region")
    entry = lax.broadcasted_iota(jnp.int32, (count, LANES), 0)
    lane = lax.broadcasted_iota(jnp.int32, (count, LANES), 1)
    picks = [
        jnp.where(entry == start + lane % width, 1.0, 0.0).astype(jnp.bfloat16)
        for start, width in ((0, count), (0, CAP), (count - CAP, CAP))
    ]
    loads[0].wait()
    cells = jnp.broadcast_to(cell_ref[...].astype(jnp.float32), (SUB, count)).astype(jnp.bfloat16)
    spread = [lax.dot_general(cells, pick, (NN, ((), ())), preferred_element_type=jnp.float32) for pick in picks]
    loads[1].wait()
    mine = sector_ref[me]
    far = me ^ half_way
    is_next = lambda first, second: second == lax.rem(first + 1, regions)
    from_left, from_right, to_right = jnp.int32(0), jnp.int32(0), []
    for step in range(1, regions):
        sector = sector_ref[me ^ step]
        from_left = jnp.where(is_next(sector, mine), step, from_left)
        from_right = jnp.where(is_next(mine, sector), step, from_right)
    codes = [from_left, from_right]
    for step in range(1, half_way):
        sector = sector_ref[me ^ step]
        to_right.append(is_next(mine, sector))
        codes.append(is_next(sector_ref[far], sector).astype(jnp.int32))
    for i, code in enumerate(codes):
        side_ref[i] = jnp.broadcast_to(code, (SUB, LANES))
    for load in loads[2:]:
        load.wait()
    half = count // SUB * members
    own_ref[0, :, :half] = folded(anom_ref[...])
    own_ref[1, :, :half] = folded(weight_ref[...])
    own_ref[0, :, half:] = spread[0]
    own_ref[1, :, half:] = spread[0]
    low = (folded(anom_ref[:CAP, :]), folded(weight_ref[:CAP, :]), spread[1])
    high = (folded(anom_ref[count - CAP :, :]), folded(weight_ref[count - CAP :, :]), spread[2])
    wide = CAP // SUB * members
    upper = lax.broadcasted_iota(jnp.int32, (SUB, LANES), 0) >= SUB // 2
    for i, (start, stop) in enumerate(((0, wide), (wide, 2 * wide), (2 * wide, 2 * wide + LANES))):
        if i < 2:
            cross_ref[:, start:stop] = low[i]
            cross_ref[:, 2 * wide + start : 2 * wide + stop] = high[i]
        for near, up in zip(near_refs, to_right):
            near[:, start:stop] = jnp.where(up, high[i], low[i])
    cross_ref[:, 4 * wide :] = jnp.where(upper, high[2], low[2])


def pair_tile(pair_ref, upper, at, width):
    if at < width - LANES:
        at += upper * (width - LANES)
        return pair_ref[:, at : at + LANES]
    row = upper * (SUB // 2)
    return jnp.broadcast_to(pair_ref[row : row + 1, pair_ref.shape[1] - LANES :], (SUB, LANES))


def relay_kernel(side_ref, cross_ref, *pass_refs):
    width = pass_refs[0].shape[1]
    for step, out in enumerate(pass_refs, start=1):
        up = side_ref[1 + step] == 1
        for at in range(0, width, LANES):
            out[:, at : at + LANES] = jnp.where(up, pair_tile(cross_ref, 1, at, width), pair_tile(cross_ref, 0, at, width))


def pick_kernel(side_ref, cross_ref, *refs):
    *slot_refs, halo_ref = refs
    width = slot_refs[0].shape[1]
    half_way = len(slot_refs) // 2 + 1
    near, passed = slot_refs[: half_way - 1], slot_refs[half_way - 1 :]
    upper = lax.broadcasted_iota(jnp.int32, (SUB, LANES), 0) >= SUB // 2
    for at in range(0, width, LANES):
        values = []
        for side in range(2):
            code = side_ref[side]
            value = pair_tile(cross_ref, 1 - side, at, width)
            for step in range(1, half_way):
                value = jnp.where(code == step, near[step - 1][:, at : at + LANES], value)
                value = jnp.where(code == step + half_way, passed[step - 1][:, at : at + LANES], value)
            values.append(value)
        if at < width - LANES:
            for side, value in enumerate(values):
                start = side * (width - LANES) + at
                halo_ref[:, start : start + LANES] = value
        else:
            halo_ref[:, 2 * at :] = jnp.where(upper, values[1], values[0])


def joined(left, right, dims):
    axis = dims[1][0]
    lefts = jnp.concatenate([left[0], left[0], left[1]], axis=1)
    rights = jnp.concatenate([right[0], right[1], right[0]], axis=axis)
    return lax.dot_general(lefts, rights, (dims, ((), ())), preferred_element_type=jnp.float32)


def prep_kernel(state_hbm, hi_ref, lo_ref, state_ref, sems):
    levels, rows = state_ref.shape[:2]
    loads = [pltpu.make_async_copy(state_hbm.at[l], state_ref.at[l], sems.at[l]) for l in range(levels)]
    for load in loads:
        load.start()
    for l in range(levels):
        loads[l].wait()
        here = pl.ds(l * rows, rows)
        hi_ref[here, :], lo_ref[here, :] = split(state_ref[l])


def own_kernel(tree, s_hi, s_lo, *refs):
    *flat, out_hbm, edge_ref, out_ref, a_hi, a_lo, w_hi, w_lo, out_sem = refs
    packs = [pack if isinstance(pack, tuple) else (pack.at[0], pack.at[1]) for pack in jax.tree.unflatten(tree, flat)]
    blocks = len(packs)
    levels, middle, members = out_ref.shape
    rows = middle + 2 * EDGE
    half = packs[0][0].shape[1] - LANES
    count = half // members * SUB
    lane = lax.broadcasted_iota(jnp.int32, (1, LANES), 1)
    for b in range(blocks):
        here = pl.ds(b * count, count)
        a_hi[here, :], a_lo[here, :] = split(unfolded(packs[b][0][:, :half], members))
    for b in range(blocks):
        here = pl.ds(b * count, count)
        w_hi[here, :], w_lo[here, :] = split(unfolded(packs[b][1][:, :half], members))
    each = LANES // count
    groups = []
    for g in range(0, blocks, each):
        cells = packs[g][0][:1, half:]
        for b in range(1, each):
            cells = jnp.where(lane >= b * count, packs[g + b][0][:1, half:], cells)
        groups.append(taper(0, rows, cells, 0) / (members - 1))
    rho = jnp.concatenate(groups, axis=1)
    stores = []
    for l in range(levels):
        here = pl.ds(l * rows, rows)
        covar = product((s_hi[here, :], s_lo[here, :]), (a_hi[...], a_lo[...]), NT) * rho
        total = product(split(covar), (w_hi[...], w_lo[...]), NN)
        out_ref[l] = total[EDGE : rows - EDGE]
        stores.append(pltpu.make_async_copy(out_ref.at[l], out_hbm.at[l, pl.ds(EDGE, middle)], out_sem.at[l]))
        stores[-1].start()
        for side, part in enumerate((slice(0, EDGE), slice(rows - EDGE, rows))):
            edge_ref[side, pl.ds(l * EDGE, EDGE), :] = total[part]
    for store in stores:
        store.wait()


def halo_kernel(blocks, total_hbm, edge_ref, s_hi, s_lo, *refs):
    halo_refs, (out_hbm, out_ref, out_sem) = refs[:blocks], refs[blocks:]
    levels, columns, members = out_hbm.shape
    wide = CAP // SUB * members
    count = blocks * CAP
    starts = (0, columns - EDGE)
    lane = lax.broadcasted_iota(jnp.int32, (1, LANES), 1)
    per = LANES // CAP
    dot = functools.partial(lax.dot_general, dimension_numbers=(NT, ((), ())), preferred_element_type=jnp.float32)
    covars, weights = [], []
    for s, shift in enumerate((-SECT_W, SECT_W)):
        at = 2 * s * wide
        anom = split(jnp.concatenate([unfolded(h[:, at : at + wide], members) for h in halo_refs], axis=0))
        both = jnp.concatenate(anom, axis=0)
        high, low = (
            jnp.concatenate([ref[l * columns + starts[s] : l * columns + starts[s] + EDGE, :] for l in range(levels)], axis=0)
            for ref in (s_hi, s_lo)
        )
        wide_dot = dot(high, both)
        covar = wide_dot[:, :count] + (wide_dot[:, count:] + dot(low, anom[0]))
        row = s * (SUB // 2)
        tiles = [h[row : row + 1, 4 * wide :] for h in halo_refs]
        groups = []
        for g in range(0, blocks, per):
            cells = tiles[g]
            for b in range(1, min(per, blocks - g)):
                cells = jnp.where(lane >= b * CAP, tiles[g + b], cells)
            groups.append(cells)
        cells = jnp.concatenate(groups, axis=1)[:, :count]
        rho = taper(starts[s], EDGE, cells, shift) / (members - 1)
        covars.append(split((covar.reshape(levels, EDGE, -1) * rho[None]).reshape(levels * EDGE, -1)))
        weights.append(split(jnp.concatenate([unfolded(h[:, at + wide : at + 2 * wide], members) for h in halo_refs], axis=0)))
    stores = []
    for s in range(2):
        out_ref[s] = edge_ref[s] + joined(covars[s], weights[s], NN)
        for l in range(levels):
            store = pltpu.make_async_copy(
                out_ref.at[s, pl.ds(l * EDGE, EDGE)], out_hbm.at[l, pl.ds(starts[s], EDGE)], out_sem.at[s, l]
            )
            store.start()
            stores.append(store)
    for store in stores:
        store.wait()


def on_device(state_anom, obs_anom, obs_weight, obs_cell, sector_of):
    f32 = jnp.float32
    regions, owners = lax.axis_size("region"), lax.axis_size("state")
    levels, columns, members = state_anom.shape[1:]
    count = obs_anom.shape[1]
    blocks = owners

    assert regions & (regions - 1) == 0
    half_way = regions // 2
    slot = jax.ShapeDtypeStruct((SUB, 2 * (CAP // SUB) * members + LANES), f32)
    pair = jax.ShapeDtypeStruct((SUB, 2 * slot.shape[1] - LANES), f32)
    near = range(1, half_way)
    own_pack, sides, cross, *slots = pl.pallas_call(
        pack_kernel,
        out_shape=[jax.ShapeDtypeStruct((2, SUB, count // SUB * members + LANES), f32)]
        + [jax.ShapeDtypeStruct((half_way + 1, SUB, LANES), jnp.int32), pair]
        + [slot] * len(near),
        in_specs=[HBM] * 4,
        out_specs=[VMEM] * (3 + len(near)),
        scratch_shapes=[
            pltpu.SMEM((regions,), jnp.int32),
            pltpu.VMEM((count, members), f32),
            pltpu.VMEM((count, members), f32),
            pltpu.VMEM((1, count), jnp.int32),
            pltpu.SemaphoreType.DMA((4,)),
        ],
        compiler_params=limit(8),
        name="pack",
    )(*in_hbm(sector_of, obs_anom, obs_weight, obs_cell))
    crossed = exchange(cross, "region", half_way)
    direct = [exchange(slots[k - 1], "region", k) for k in near]
    relayed = pl.pallas_call(
        relay_kernel,
        out_shape=[slot] * len(near),
        in_specs=[VMEM] * 2,
        out_specs=[VMEM] * len(near),
        compiler_params=limit(4),
        name="relay",
    )(sides, crossed)
    passed = [exchange(relayed[k - 1], "region", k) for k in near]
    packs = gather(own_pack, "state")
    halo = pl.pallas_call(
        pick_kernel,
        out_shape=pair,
        in_specs=[VMEM] * (2 + 2 * len(near)),
        out_specs=VMEM,
        compiler_params=limit(4),
        name="pick",
    )(sides, crossed, *direct, *passed)
    halos = [halo] + [exchange(halo, "state", k) for k in range(1, owners)]

    obs = blocks * count
    state = state_anom[0]
    bf16 = jnp.bfloat16
    middle = columns - 2 * EDGE
    edges = (2, levels * EDGE, members)
    halves = (levels * columns, members)
    s_hi, s_lo = pl.pallas_call(
        prep_kernel,
        out_shape=[jax.ShapeDtypeStruct(halves, bf16)] * 2,
        in_specs=[HBM],
        out_specs=[VMEM] * 2,
        scratch_shapes=[pltpu.VMEM(state.shape, f32), pltpu.SemaphoreType.DMA((levels,))],
        compiler_params=limit(8),
        name="prep",
    )(*in_hbm(state))
    flat, tree = jax.tree.flatten(packs)
    total, edge = pl.pallas_call(
        functools.partial(own_kernel, tree),
        out_shape=[jax.ShapeDtypeStruct(state.shape, f32), jax.ShapeDtypeStruct(edges, f32)],
        in_specs=[VMEM] * (2 + len(flat)),
        out_specs=[HBM, VMEM],
        scratch_shapes=[pltpu.VMEM((levels, middle, members), f32)]
        + [pltpu.VMEM((obs, members), bf16)] * 4
        + [pltpu.SemaphoreType.DMA((levels,))],
        cost_estimate=pl.CostEstimate(
            flops=12 * levels * columns * obs * members, bytes_accessed=8 * state.size + 8 * obs * members, transcendentals=0
        ),
        compiler_params=limit(24),
        name="own",
    )(s_hi, s_lo, *flat)
    out = pl.pallas_call(
        functools.partial(halo_kernel, blocks),
        out_shape=jax.ShapeDtypeStruct(state.shape, f32),
        in_specs=[HBM] + [VMEM] * (3 + blocks),
        out_specs=HBM,
        scratch_shapes=[pltpu.VMEM(edges, f32), pltpu.SemaphoreType.DMA((2, levels))],
        input_output_aliases={0: 0},
        compiler_params=limit(16),
        name="halo",
    )(total, edge, s_hi, s_lo, *halos)
    return out[None]


def solution(mesh):
    in_specs = (
        P("region", "state", None, None),
        P("region", "state", None),
        P("region", "state", None),
        P("region", "state"),
        P(),
    )
    out_specs = P("region", "state", None, None)
    return jax.shard_map(on_device, mesh=mesh, in_specs=in_specs, out_specs=out_specs, check_vma=False)
```

profile of v0, /device:TPU:0, one launch (start us, length us, event | category | flops | bytes accessed | tf_op | source)
XLA Modules:
  0.0 37.7 jit_solution(4278893018545443805)
XLA Ops:
  0.0 1.1 %pack.1 = (f32[2,8,4224]{2,1,0:T(8,128)S(1)}, s32[5,8,128]{2,1,0:T(8,128)S(1)}, f32[8,4224]{1,0:T(8,128)S(1)}, f32[8,2176]{1,0:T(8,128)S(1)}, f32[8,2176]{1,0:T(8,128)S(1)}, /*index=5*/f32[8,2176]{1,0:T(8,128)S(1)}) custom-call(s32[8]{0:T(128)} %sector_hbm.1, f32[1,64,512]{2,1,0:T(8,128)} %anom_hbm.1, f32[1,64,512]{2,1,0:T(8,128)} %weight_hbm.1, ...), custom_call_target="tpu_custom_call" | custom-call | tf_op jit(solution)/shard_map/pack/pallas_call | solution.py:301
  1.1 3.1 %collective-permute-start.1 = (f32[2,8,4224]{2,1,0:T(8,128)S(1)}, f32[2,8,4224]{2,1,0:T(8,128)S(1)}, u32[]{:S(2)}, u32[]{:S(2)}) collective-permute-start(f32[2,8,4224]{2,1,0:T(8,128)S(1)} %get-tuple-element.20.refs_0_), channel_id=1, source_target_pairs={{0,2},{1,3},{2,0},{3,1},{4,6},{5,7},{6,4},{7,5},{8,10},{9,11},{10,... | collective-permute-start | bytes 811016 | tf_op jit(solution)/shard_map/ppermute | solution.py:37
  4.1 1.5 %collective-permute-start = (f32[2,8,4224]{2,1,0:T(8,128)S(1)}, f32[2,8,4224]{2,1,0:T(8,128)S(1)}, u32[]{:S(2)}, u32[]{:S(2)}) collective-permute-start(f32[2,8,4224]{2,1,0:T(8,128)S(1)} %get-tuple-element.20.refs_0_), channel_id=1, source_target_pairs={{0,1},{1,0},{2,3},{3,2},{4,5},{5,4},{6,7},{7,6},{8,9},{9,8},{10,11... | collective-permute-start | bytes 811016 | tf_op jit(solution)/shard_map/ppermute | solution.py:37
  5.6 0.0 collective-permute-start.5
  5.6 1.6 %collective-permute-start.6 = (f32[8,2176]{1,0:T(8,128)S(1)}, f32[8,2176]{1,0:T(8,128)S(1)}, u32[]{:S(2)}, u32[]{:S(2)}) collective-permute-start(f32[8,2176]{1,0:T(8,128)S(1)} %get-tuple-element.26), channel_id=1, source_target_pairs={{0,8},{4,12},{8,0},{12,4},{16,24},{20,28},{24,16},{28,20},{1,9},{5... | collective-permute-start | bytes 208904 | tf_op jit(solution)/shard_map/ppermute | solution.py:37
  7.2 0.3 collective-permute-start.7
  7.5 3.1 %collective-permute-done.1.refs_2_ = f32[2,8,4224]{2,1,0:T(8,128)S(1)} collective-permute-done((f32[2,8,4224]{2,1,0:T(8,128)S(1)}, f32[2,8,4224]{2,1,0:T(8,128)S(1)}, u32[]{:S(2)}, u32[]{:S(2)}) %collective-permute-start.1) | collective-permute-done | bytes 270368 | tf_op jit(solution)/shard_map/ppermute | solution.py:37
  10.6 2.8 %collective-permute-start.4 = (f32[8,4224]{1,0:T(8,128)S(1)}, f32[8,4224]{1,0:T(8,128)S(1)}, u32[]{:S(2)}, u32[]{:S(2)}) collective-permute-start(f32[8,4224]{1,0:T(8,128)S(1)} %get-tuple-element.24), channel_id=1, source_target_pairs={{0,16},{4,20},{8,24},{12,28},{16,0},{20,4},{24,8},{28,12},{1,17},{... | collective-permute-start | bytes 405512 | tf_op jit(solution)/shard_map/ppermute | solution.py:37
  13.4 1.6 %collective-permute-start.3 = (f32[8,4224]{1,0:T(8,128)S(1)}, f32[8,4224]{1,0:T(8,128)S(1)}, u32[]{:S(2)}, u32[]{:S(2)}) collective-permute-start(f32[8,4224]{1,0:T(8,128)S(1)} %slice_bitcast_fusion), channel_id=1, source_target_pairs={{0,1},{1,0},{2,3},{3,2},{4,5},{5,4},{6,7},{7,6},{8,9},{9,8},{10,11... | collective-permute-start | bytes 405512 | tf_op jit(solution)/shard_map/ppermute | solution.py:37
  15.0 4.1 %collective-permute-done.4.cross_ref = f32[8,4224]{1,0:T(8,128)S(1)} collective-permute-done((f32[8,4224]{1,0:T(8,128)S(1)}, f32[8,4224]{1,0:T(8,128)S(1)}, u32[]{:S(2)}, u32[]{:S(2)}) %collective-permute-start.4) | collective-permute-done | bytes 135200 | tf_op jit(solution)/shard_map/ppermute | solution.py:37
  19.2 1.5 %collective-permute-start.2 = (f32[8,4224]{1,0:T(8,128)S(1)}, f32[8,4224]{1,0:T(8,128)S(1)}, u32[]{:S(2)}, u32[]{:S(2)}) collective-permute-start(f32[8,4224]{1,0:T(8,128)S(1)} %slice_bitcast_fusion.1), channel_id=1, source_target_pairs={{0,2},{1,3},{2,0},{3,1},{4,6},{5,7},{6,4},{7,5},{8,10},{9,11},{10,... | collective-permute-start | bytes 405512 | tf_op jit(solution)/shard_map/ppermute | solution.py:37
  20.6 0.1 collective-permute-start.8
  20.7 0.7 %collective-permute-start.9 = (f32[8,2176]{1,0:T(8,128)S(1)}, f32[8,2176]{1,0:T(8,128)S(1)}, u32[]{:S(2)}, u32[]{:S(2)}) collective-permute-start(f32[8,2176]{1,0:T(8,128)S(1)} %get-tuple-element.29), channel_id=1, source_target_pairs={{0,8},{4,12},{8,0},{12,4},{16,24},{20,28},{24,16},{28,20},{1,9},{5... | collective-permute-start | bytes 208904 | tf_op jit(solution)/shard_map/ppermute | solution.py:37
  21.5 1.1 %collective-permute-start.10 = (f32[8,2176]{1,0:T(8,128)S(1)}, f32[8,2176]{1,0:T(8,128)S(1)}, u32[]{:S(2)}, u32[]{:S(2)}) collective-permute-start(f32[8,2176]{1,0:T(8,128)S(1)} %get-tuple-element.30), channel_id=1, source_target_pairs={{0,12},{4,8},{8,4},{12,0},{16,28},{20,24},{24,20},{28,16},{1,13},{... | collective-permute-start | bytes 208904 | tf_op jit(solution)/shard_map/ppermute | solution.py:37
  22.6 1.6 %prep.1 = (bf16[1024,512]{1,0:T(8,128)(2,1)S(1)}, bf16[1024,512]{1,0:T(8,128)(2,1)S(1)}) custom-call(f32[4,256,512]{2,1,0:T(8,128)} %bitcast.6), custom_call_target="tpu_custom_call" | custom-call | tf_op jit(solution)/shard_map/prep/pallas_call | solution.py:346
  24.2 1.6 %collective-permute-done.9.refs_4_ = f32[8,2176]{1,0:T(8,128)S(1)} collective-permute-done((f32[8,2176]{1,0:T(8,128)S(1)}, f32[8,2176]{1,0:T(8,128)S(1)}, u32[]{:S(2)}, u32[]{:S(2)}) %collective-permute-start.9) | collective-permute-done | bytes 69664 | tf_op jit(solution)/shard_map/ppermute | solution.py:37
  25.9 0.4 %collective-permute-done.10.refs_5_ = f32[8,2176]{1,0:T(8,128)S(1)} collective-permute-done((f32[8,2176]{1,0:T(8,128)S(1)}, f32[8,2176]{1,0:T(8,128)S(1)}, u32[]{:S(2)}, u32[]{:S(2)}) %collective-permute-start.10) | collective-permute-done | bytes 69664 | tf_op jit(solution)/shard_map/ppermute | solution.py:37
  26.3 1.5 %collective-permute-start.13 = (f32[8,4224]{1,0:T(8,128)S(1)}, f32[8,4224]{1,0:T(8,128)S(1)}, u32[]{:S(2)}, u32[]{:S(2)}) collective-permute-start(f32[8,4224]{1,0:T(8,128)S(1)} %pick.1.refs_0_), channel_id=1, source_target_pairs={{0,3},{1,2},{2,1},{3,0},{4,7},{5,6},{6,5},{7,4},{8,11},{9,10},{10,... | collective-permute-start | bytes 405512 | tf_op jit(solution)/shard_map/ppermute | solution.py:37
  27.8 1.5 %collective-permute-start.12 = (f32[8,4224]{1,0:T(8,128)S(1)}, f32[8,4224]{1,0:T(8,128)S(1)}, u32[]{:S(2)}, u32[]{:S(2)}) collective-permute-start(f32[8,4224]{1,0:T(8,128)S(1)} %pick.1.refs_0_), channel_id=1, source_target_pairs={{0,2},{1,3},{2,0},{3,1},{4,6},{5,7},{6,4},{7,5},{8,10},{9,11},{10,... | collective-permute-start | bytes 405512 | tf_op jit(solution)/shard_map/ppermute | solution.py:37
  29.3 0.5 %collective-permute-start.11 = (f32[8,4224]{1,0:T(8,128)S(1)}, f32[8,4224]{1,0:T(8,128)S(1)}, u32[]{:S(2)}, u32[]{:S(2)}) collective-permute-start(f32[8,4224]{1,0:T(8,128)S(1)} %pick.1.refs_0_), channel_id=1, source_target_pairs={{0,1},{1,0},{2,3},{3,2},{4,5},{5,4},{6,7},{7,6},{8,9},{9,8},{10,11... | collective-permute-start | bytes 405512 | tf_op jit(solution)/shard_map/ppermute | solution.py:37
  29.9 3.8 %own.1 = (f32[4,256,512]{2,1,0:T(8,128)}, f32[2,256,512]{2,1,0:T(8,128)S(1)}) custom-call(bf16[1024,512]{1,0:T(8,128)(2,1)S(1)} %get-tuple-element.18.s_hi, bf16[1024,512]{1,0:T(8,128)(2,1)S(1)} %get-tuple-element.19.s_lo, f32[2,8,4224]{2,1,0:T(8,128)S(1)} %get-tuple-element.20.refs_0_, f32[2,8,4224]{2,1,0:T(8,128)S(1)} %collective-permute-done.refs_1_, ...), custom_call_target="tpu_custom_call" | custom-call | flops 1610612736 | bytes 5242880 | tf_op jit(solution)/shard_map/own/pallas_call | solution.py:356
  33.6 0.1 collective-permute-done.13.refs_3_
  33.8 2.3 %collective-permute-done.12.refs_2_ = f32[8,4224]{1,0:T(8,128)S(1)} collective-permute-done((f32[8,4224]{1,0:T(8,128)S(1)}, f32[8,4224]{1,0:T(8,128)S(1)}, u32[]{:S(2)}, u32[]{:S(2)}) %collective-permute-start.12) | collective-permute-done | bytes 135200 | tf_op jit(solution)/shard_map/ppermute | solution.py:37
  36.0 1.7 %halo.1 = f32[4,256,512]{2,1,0:T(8,128)} custom-call(f32[4,256,512]{2,1,0:T(8,128)} %get-tuple-element.21.total_hbm, f32[2,256,512]{2,1,0:T(8,128)S(1)} %get-tuple-element.22.edge_ref, bf16[1024,512]{1,0:T(8,128)(2,1)S(1)} %get-tuple-element.18.s_hi, bf16[1024,512]{1,0:T(8,128)(2,1)S(1)} %get-tuple-element.19.s_lo, ...), custom_call_target="tpu_custom_call", output_to_operand_aliasing={{}: (0, {})} | custom-call | tf_op jit(solution)/shard_map/halo/pallas_call | solution.py:370
  (12 shorter events, 0.1 us)
Async XLA Ops:
  1.1 9.5 %collective-permute-start.1 = (f32[2,8,4224]{2,1,0:T(8,128)S(1)}, f32[2,8,4224]{2,1,0:T(8,128)S(1)}, u32[]{:S(2)}, u32[]{:S(2)}) collective-permute-start(f32[2,8,4224]{2,1,0:T(8,128)S(1)} %get-tuple-element.20.refs_0_), channel_id=1, source_target_pairs={{0,2},{1,3},{2,0},{3,1},{4,6},{5,7},{6,4},{7,5},{8,10},{9,11},{10,... | collective-permute-start | bytes 811016 | tf_op jit(solution)/shard_map/ppermute | solution.py:37
  4.1 9.3 %collective-permute-start = (f32[2,8,4224]{2,1,0:T(8,128)S(1)}, f32[2,8,4224]{2,1,0:T(8,128)S(1)}, u32[]{:S(2)}, u32[]{:S(2)}) collective-permute-start(f32[2,8,4224]{2,1,0:T(8,128)S(1)} %get-tuple-element.20.refs_0_), channel_id=1, source_target_pairs={{0,1},{1,0},{2,3},{3,2},{4,5},{5,4},{6,7},{7,6},{8,9},{9,8},{10,11... | collective-permute-start | bytes 811016 | tf_op jit(solution)/shard_map/ppermute | solution.py:37
  5.6 15.0 %collective-permute-start.5 = (f32[8,2176]{1,0:T(8,128)S(1)}, f32[8,2176]{1,0:T(8,128)S(1)}, u32[]{:S(2)}, u32[]{:S(2)}) collective-permute-start(f32[8,2176]{1,0:T(8,128)S(1)} %get-tuple-element.25), channel_id=1, source_target_pairs={{0,4},{4,0},{8,12},{12,8},{16,20},{20,16},{24,28},{28,24},{1,5},{5... | collective-permute-start | bytes 208904 | tf_op jit(solution)/shard_map/ppermute | solution.py:37
  5.6 15.1 %collective-permute-start.6 = (f32[8,2176]{1,0:T(8,128)S(1)}, f32[8,2176]{1,0:T(8,128)S(1)}, u32[]{:S(2)}, u32[]{:S(2)}) collective-permute-start(f32[8,2176]{1,0:T(8,128)S(1)} %get-tuple-element.26), channel_id=1, source_target_pairs={{0,8},{4,12},{8,0},{12,4},{16,24},{20,28},{24,16},{28,20},{1,9},{5... | collective-permute-start | bytes 208904 | tf_op jit(solution)/shard_map/ppermute | solution.py:37
  7.2 14.3 %collective-permute-start.7 = (f32[8,2176]{1,0:T(8,128)S(1)}, f32[8,2176]{1,0:T(8,128)S(1)}, u32[]{:S(2)}, u32[]{:S(2)}) collective-permute-start(f32[8,2176]{1,0:T(8,128)S(1)} %get-tuple-element.27), channel_id=1, source_target_pairs={{0,12},{4,8},{8,4},{12,0},{16,28},{20,24},{24,20},{28,16},{1,13},{... | collective-permute-start | bytes 208904 | tf_op jit(solution)/shard_map/ppermute | solution.py:37
  10.6 8.5 %collective-permute-start.4 = (f32[8,4224]{1,0:T(8,128)S(1)}, f32[8,4224]{1,0:T(8,128)S(1)}, u32[]{:S(2)}, u32[]{:S(2)}) collective-permute-start(f32[8,4224]{1,0:T(8,128)S(1)} %get-tuple-element.24), channel_id=1, source_target_pairs={{0,16},{4,20},{8,24},{12,28},{16,0},{20,4},{24,8},{28,12},{1,17},{... | collective-permute-start | bytes 405512 | tf_op jit(solution)/shard_map/ppermute | solution.py:37
  13.4 16.4 %collective-permute-start.3 = (f32[8,4224]{1,0:T(8,128)S(1)}, f32[8,4224]{1,0:T(8,128)S(1)}, u32[]{:S(2)}, u32[]{:S(2)}) collective-permute-start(f32[8,4224]{1,0:T(8,128)S(1)} %slice_bitcast_fusion), channel_id=1, source_target_pairs={{0,1},{1,0},{2,3},{3,2},{4,5},{5,4},{6,7},{7,6},{8,9},{9,8},{10,11... | collective-permute-start | bytes 405512 | tf_op jit(solution)/shard_map/ppermute | solution.py:37
  19.2 10.7 %collective-permute-start.2 = (f32[8,4224]{1,0:T(8,128)S(1)}, f32[8,4224]{1,0:T(8,128)S(1)}, u32[]{:S(2)}, u32[]{:S(2)}) collective-permute-start(f32[8,4224]{1,0:T(8,128)S(1)} %slice_bitcast_fusion.1), channel_id=1, source_target_pairs={{0,2},{1,3},{2,0},{3,1},{4,6},{5,7},{6,4},{7,5},{8,10},{9,11},{10,... | collective-permute-start | bytes 405512 | tf_op jit(solution)/shard_map/ppermute | solution.py:37
  20.6 3.6 %collective-permute-start.8 = (f32[8,2176]{1,0:T(8,128)S(1)}, f32[8,2176]{1,0:T(8,128)S(1)}, u32[]{:S(2)}, u32[]{:S(2)}) collective-permute-start(f32[8,2176]{1,0:T(8,128)S(1)} %get-tuple-element.28), channel_id=1, source_target_pairs={{0,4},{4,0},{8,12},{12,8},{16,20},{20,16},{24,28},{28,24},{1,5},{5... | collective-permute-start | bytes 208904 | tf_op jit(solution)/shard_map/ppermute | solution.py:37
  20.7 5.1 %collective-permute-start.9 = (f32[8,2176]{1,0:T(8,128)S(1)}, f32[8,2176]{1,0:T(8,128)S(1)}, u32[]{:S(2)}, u32[]{:S(2)}) collective-permute-start(f32[8,2176]{1,0:T(8,128)S(1)} %get-tuple-element.29), channel_id=1, source_target_pairs={{0,8},{4,12},{8,0},{12,4},{16,24},{20,28},{24,16},{28,20},{1,9},{5... | collective-permute-start | bytes 208904 | tf_op jit(solution)/shard_map/ppermute | solution.py:37
  21.5 4.8 %collective-permute-start.10 = (f32[8,2176]{1,0:T(8,128)S(1)}, f32[8,2176]{1,0:T(8,128)S(1)}, u32[]{:S(2)}, u32[]{:S(2)}) collective-permute-start(f32[8,2176]{1,0:T(8,128)S(1)} %get-tuple-element.30), channel_id=1, source_target_pairs={{0,12},{4,8},{8,4},{12,0},{16,28},{20,24},{24,20},{28,16},{1,13},{... | collective-permute-start | bytes 208904 | tf_op jit(solution)/shard_map/ppermute | solution.py:37
  26.3 7.5 %collective-permute-start.13 = (f32[8,4224]{1,0:T(8,128)S(1)}, f32[8,4224]{1,0:T(8,128)S(1)}, u32[]{:S(2)}, u32[]{:S(2)}) collective-permute-start(f32[8,4224]{1,0:T(8,128)S(1)} %pick.1.refs_0_), channel_id=1, source_target_pairs={{0,3},{1,2},{2,1},{3,0},{4,7},{5,6},{6,5},{7,4},{8,11},{9,10},{10,... | collective-permute-start | bytes 405512 | tf_op jit(solution)/shard_map/ppermute | solution.py:37
  27.8 8.2 %collective-permute-start.12 = (f32[8,4224]{1,0:T(8,128)S(1)}, f32[8,4224]{1,0:T(8,128)S(1)}, u32[]{:S(2)}, u32[]{:S(2)}) collective-permute-start(f32[8,4224]{1,0:T(8,128)S(1)} %pick.1.refs_0_), channel_id=1, source_target_pairs={{0,2},{1,3},{2,0},{3,1},{4,6},{5,7},{6,4},{7,5},{8,10},{9,11},{10,... | collective-permute-start | bytes 405512 | tf_op jit(solution)/shard_map/ppermute | solution.py:37
  29.3 6.7 %collective-permute-start.11 = (f32[8,4224]{1,0:T(8,128)S(1)}, f32[8,4224]{1,0:T(8,128)S(1)}, u32[]{:S(2)}, u32[]{:S(2)}) collective-permute-start(f32[8,4224]{1,0:T(8,128)S(1)} %pick.1.refs_0_), channel_id=1, source_target_pairs={{0,1},{1,0},{2,3},{3,2},{4,5},{5,4},{6,7},{7,6},{8,9},{9,8},{10,11... | collective-permute-start | bytes 405512 | tf_op jit(solution)/shard_map/ppermute | solution.py:37
where the time goes:
time: 37.9 us; the launch traced here: 37.7 us
  starting transfers between devices  17.7 us (47%)
  waiting for transfers between devices  11.7 us (31%)
  Pallas kernels  8.23 us (22%)
    ppermute x14, starting transfers between devices, exchange(): lax.ppermute(value, axis, [(i, target(i, step, size)) for i in range(size)])  17.7 us
    ppermute x14, waiting for transfers between devices, exchange(): lax.ppermute(value, axis, [(i, target(i, step, size)) for i in range(size)])  11.7 us
    pallas_call x1, Pallas kernels, on_device(): pl.pallas_call(functools.partial(own_kernel, tree), out_shape=[jax.ShapeD...  3.75 us
    pallas_call x1, Pallas kernels, on_device(): pl.pallas_call(functools.partial(halo_kernel, blocks), out_shape=jax.Shap...  1.72 us
    pallas_call x1, Pallas kernels, on_device(): pl.pallas_call(prep_kernel, out_shape=[jax.ShapeDtypeStruct(halves, bf16)...  1.64 us
    pallas_call x1, Pallas kernels, on_device(): pl.pallas_call(pack_kernel, out_shape=[jax.ShapeDtypeStruct((2, SUB, coun...  1.06 us
  transfers between devices with their start and end apart: 14, of which 6 were waited for; matrix products, arithmetic and copies ran while one was open for 0% of the time, Pallas kernels for 14%

commit v1 on v0

--- a/solution.py
+++ b/solution.py
@@ -32,17 +32,22 @@
     return index ^ step if size & (size - 1) == 0 else (index + step) % size
 
 
-def exchange(value, axis, step):
+def exchange(value, axis, step, ring=False):
     size = lax.axis_size(axis)
-    return lax.ppermute(value, axis, [(i, target(i, step, size)) for i in range(size)])
+    pairs = [(i, target(i, step, size)) for i in range(size)]
+    if ring and size == 4 and step < 3:
+        around = (0, 1, 3, 2)
+        by = 1 if step == 1 else 3
+        pairs = [(around[i], around[(i + by) % 4]) for i in range(4)]
+    return lax.ppermute(value, axis, pairs)
 
 
 def gather(value, axis):
     size = lax.axis_size(axis)
     steps = (2, 1) if size == 4 else range(size - 1, 0, -1)
-    got = {step: exchange(value, axis, step) for step in steps}
+    got = {step: exchange(value, axis, step, ring=True) for step in steps}
     if size == 4:
-        got[3] = [exchange(got[1][0], axis, 2), exchange(got[2][1], axis, 1)]
+        got[3] = [exchange(got[k][k - 1], axis, k, ring=True) for k in (1, 2)]
     return [(half[0], half[1]) if isinstance(half, list) else half for half in [value] + [got[k] for k in range(1, size)]]
 
 
@@ -335,7 +340,7 @@
         compiler_params=limit(4),
         name="pick",
     )(sides, crossed, *direct, *passed)
-    halos = [halo] + [exchange(halo, "state", k) for k in range(1, owners)]
+    halos = [halo] + [exchange(halo, "state", k, ring=True) for k in range(1, owners)]
 
     obs = blocks * count
     state = state_anom[0]

time: 37.9 us -> 37.9 us (level)
  waiting for transfers between devices: 11.7 us -> 12.8 us
  starting transfers between devices: 17.7 us -> 16.6 us
    ppermute x14, starting transfers between devices: 17.7 us -> 16.6 us  [exchange(): return lax.ppermute(value, axis, pairs)]
    ppermute x14, waiting for transfers between devices: 11.7 us -> 12.8 us  [exchange(): return lax.ppermute(value, axis, pairs)]
  transfers between devices with their start and end apart: 14 -> 14, of which waited for: 6 -> 7; matrix products, arithmetic and copies ran while one was open for 0% -> 0% of each run, Pallas kernels for 14% -> 14%
where the time goes in v1:
time: 37.9 us; the launch traced here: 37.7 us
  starting transfers between devices  16.6 us (44%)
  waiting for transfers between devices  12.8 us (34%)
  Pallas kernels  8.24 us (22%)
    ppermute x14, starting transfers between devices, exchange(): return lax.ppermute(value, axis, pairs)  16.6 us
    ppermute x14, waiting for transfers between devices, exchange(): return lax.ppermute(value, axis, pairs)  12.8 us
    pallas_call x1, Pallas kernels, on_device(): pl.pallas_call(functools.partial(own_kernel, tree), out_shape=[jax.ShapeD...  3.75 us
    pallas_call x1, Pallas kernels, on_device(): pl.pallas_call(functools.partial(halo_kernel, blocks), out_shape=jax.Shap...  1.72 us
    pallas_call x1, Pallas kernels, on_device(): pl.pallas_call(prep_kernel, out_shape=[jax.ShapeDtypeStruct(halves, bf16)...  1.64 us
    pallas_call x1, Pallas kernels, on_device(): pl.pallas_call(pack_kernel, out_shape=[jax.ShapeDtypeStruct((2, SUB, coun...  1.06 us
  transfers between devices with their start and end apart: 14, of which 7 were waited for; matrix products, arithmetic and copies ran while one was open for 0% of the time, Pallas kernels for 14%

profile of v1, /device:TPU:0, one launch (start us, length us, event | category | flops | bytes accessed | tf_op | source)
XLA Modules:
  0.0 37.7 jit_solution(1324512298030419350)
XLA Ops:
  0.0 1.1 %pack.1 = (f32[2,8,4224]{2,1,0:T(8,128)S(1)}, s32[5,8,128]{2,1,0:T(8,128)S(1)}, f32[8,4224]{1,0:T(8,128)S(1)}, f32[8,2176]{1,0:T(8,128)S(1)}, f32[8,2176]{1,0:T(8,128)S(1)}, /*index=5*/f32[8,2176]{1,0:T(8,128)S(1)}) custom-call(s32[8]{0:T(128)} %sector_hbm.1, f32[1,64,512]{2,1,0:T(8,128)} %anom_hbm.1, f32[1,64,512]{2,1,0:T(8,128)} %weight_hbm.1, ...), custom_call_target="tpu_custom_call" | custom-call | tf_op jit(solution)/shard_map/pack/pallas_call | solution.py:306
  1.1 3.0 %collective-permute-start.1 = (f32[2,8,4224]{2,1,0:T(8,128)S(1)}, f32[2,8,4224]{2,1,0:T(8,128)S(1)}, u32[]{:S(2)}, u32[]{:S(2)}) collective-permute-start(f32[2,8,4224]{2,1,0:T(8,128)S(1)} %get-tuple-element.20.refs_0_), channel_id=1, source_target_pairs={{0,2},{1,0},{3,1},{2,3},{4,6},{5,4},{7,5},{6,7},{8,10},{9,8},{11,9... | collective-permute-start | bytes 811016 | tf_op jit(solution)/shard_map/ppermute | solution.py:42
  4.1 0.0 collective-permute-start
  4.2 2.0 %collective-permute-start.6 = (f32[8,2176]{1,0:T(8,128)S(1)}, f32[8,2176]{1,0:T(8,128)S(1)}, u32[]{:S(2)}, u32[]{:S(2)}) collective-permute-start(f32[8,2176]{1,0:T(8,128)S(1)} %get-tuple-element.26), channel_id=1, source_target_pairs={{0,8},{4,12},{8,0},{12,4},{16,24},{20,28},{24,16},{28,20},{1,9},{5... | collective-permute-start | bytes 208904 | tf_op jit(solution)/shard_map/ppermute | solution.py:42
  6.2 0.1 collective-permute-start.7
  6.3 4.3 %collective-permute-done.1.refs_2_ = f32[2,8,4224]{2,1,0:T(8,128)S(1)} collective-permute-done((f32[2,8,4224]{2,1,0:T(8,128)S(1)}, f32[2,8,4224]{2,1,0:T(8,128)S(1)}, u32[]{:S(2)}, u32[]{:S(2)}) %collective-permute-start.1) | collective-permute-done | bytes 270368 | tf_op jit(solution)/shard_map/ppermute | solution.py:42
  10.6 2.8 %collective-permute-start.4 = (f32[8,4224]{1,0:T(8,128)S(1)}, f32[8,4224]{1,0:T(8,128)S(1)}, u32[]{:S(2)}, u32[]{:S(2)}) collective-permute-start(f32[8,4224]{1,0:T(8,128)S(1)} %get-tuple-element.24), channel_id=1, source_target_pairs={{0,16},{4,20},{8,24},{12,28},{16,0},{20,4},{24,8},{28,12},{1,17},{... | collective-permute-start | bytes 405512 | tf_op jit(solution)/shard_map/ppermute | solution.py:42
  13.4 1.6 %collective-permute-start.3 = (f32[8,4224]{1,0:T(8,128)S(1)}, f32[8,4224]{1,0:T(8,128)S(1)}, u32[]{:S(2)}, u32[]{:S(2)}) collective-permute-start(f32[8,4224]{1,0:T(8,128)S(1)} %slice_bitcast_fusion), channel_id=1, source_target_pairs={{0,2},{1,0},{3,1},{2,3},{4,6},{5,4},{7,5},{6,7},{8,10},{9,8},{11,9... | collective-permute-start | bytes 405512 | tf_op jit(solution)/shard_map/ppermute | solution.py:42
  15.0 4.1 %collective-permute-done.4.cross_ref = f32[8,4224]{1,0:T(8,128)S(1)} collective-permute-done((f32[8,4224]{1,0:T(8,128)S(1)}, f32[8,4224]{1,0:T(8,128)S(1)}, u32[]{:S(2)}, u32[]{:S(2)}) %collective-permute-start.4) | collective-permute-done | bytes 135200 | tf_op jit(solution)/shard_map/ppermute | solution.py:42
  19.1 1.5 %collective-permute-start.2 = (f32[8,4224]{1,0:T(8,128)S(1)}, f32[8,4224]{1,0:T(8,128)S(1)}, u32[]{:S(2)}, u32[]{:S(2)}) collective-permute-start(f32[8,4224]{1,0:T(8,128)S(1)} %slice_bitcast_fusion.1), channel_id=1, source_target_pairs={{0,1},{1,3},{3,2},{2,0},{4,5},{5,7},{7,6},{6,4},{8,9},{9,11},{11,1... | collective-permute-start | bytes 405512 | tf_op jit(solution)/shard_map/ppermute | solution.py:42
  20.6 0.1 collective-permute-start.8
  20.7 0.7 %collective-permute-start.9 = (f32[8,2176]{1,0:T(8,128)S(1)}, f32[8,2176]{1,0:T(8,128)S(1)}, u32[]{:S(2)}, u32[]{:S(2)}) collective-permute-start(f32[8,2176]{1,0:T(8,128)S(1)} %get-tuple-element.29), channel_id=1, source_target_pairs={{0,8},{4,12},{8,0},{12,4},{16,24},{20,28},{24,16},{28,20},{1,9},{5... | collective-permute-start | bytes 208904 | tf_op jit(solution)/shard_map/ppermute | solution.py:42
  21.4 1.1 %collective-permute-start.10 = (f32[8,2176]{1,0:T(8,128)S(1)}, f32[8,2176]{1,0:T(8,128)S(1)}, u32[]{:S(2)}, u32[]{:S(2)}) collective-permute-start(f32[8,2176]{1,0:T(8,128)S(1)} %get-tuple-element.30), channel_id=1, source_target_pairs={{0,12},{4,8},{8,4},{12,0},{16,28},{20,24},{24,20},{28,16},{1,13},{... | collective-permute-start | bytes 208904 | tf_op jit(solution)/shard_map/ppermute | solution.py:42
  22.5 1.6 %prep.1 = (bf16[1024,512]{1,0:T(8,128)(2,1)S(1)}, bf16[1024,512]{1,0:T(8,128)(2,1)S(1)}) custom-call(f32[4,256,512]{2,1,0:T(8,128)} %bitcast.6), custom_call_target="tpu_custom_call" | custom-call | tf_op jit(solution)/shard_map/prep/pallas_call | solution.py:351
  24.2 1.6 %collective-permute-done.9.refs_4_ = f32[8,2176]{1,0:T(8,128)S(1)} collective-permute-done((f32[8,2176]{1,0:T(8,128)S(1)}, f32[8,2176]{1,0:T(8,128)S(1)}, u32[]{:S(2)}, u32[]{:S(2)}) %collective-permute-start.9) | collective-permute-done | bytes 69664 | tf_op jit(solution)/shard_map/ppermute | solution.py:42
  25.8 0.4 %collective-permute-done.10.refs_5_ = f32[8,2176]{1,0:T(8,128)S(1)} collective-permute-done((f32[8,2176]{1,0:T(8,128)S(1)}, f32[8,2176]{1,0:T(8,128)S(1)}, u32[]{:S(2)}, u32[]{:S(2)}) %collective-permute-start.10) | collective-permute-done | bytes 69664 | tf_op jit(solution)/shard_map/ppermute | solution.py:42
  26.3 1.6 %collective-permute-start.13 = (f32[8,4224]{1,0:T(8,128)S(1)}, f32[8,4224]{1,0:T(8,128)S(1)}, u32[]{:S(2)}, u32[]{:S(2)}) collective-permute-start(f32[8,4224]{1,0:T(8,128)S(1)} %pick.1.refs_0_), channel_id=1, source_target_pairs={{0,3},{1,2},{2,1},{3,0},{4,7},{5,6},{6,5},{7,4},{8,11},{9,10},{10,... | collective-permute-start | bytes 405512 | tf_op jit(solution)/shard_map/ppermute | solution.py:42
  27.8 1.5 %collective-permute-start.12 = (f32[8,4224]{1,0:T(8,128)S(1)}, f32[8,4224]{1,0:T(8,128)S(1)}, u32[]{:S(2)}, u32[]{:S(2)}) collective-permute-start(f32[8,4224]{1,0:T(8,128)S(1)} %pick.1.refs_0_), channel_id=1, source_target_pairs={{0,2},{1,0},{3,1},{2,3},{4,6},{5,4},{7,5},{6,7},{8,10},{9,8},{11,9... | collective-permute-start | bytes 405512 | tf_op jit(solution)/shard_map/ppermute | solution.py:42
  29.3 0.5 %collective-permute-start.11 = (f32[8,4224]{1,0:T(8,128)S(1)}, f32[8,4224]{1,0:T(8,128)S(1)}, u32[]{:S(2)}, u32[]{:S(2)}) collective-permute-start(f32[8,4224]{1,0:T(8,128)S(1)} %pick.1.refs_0_), channel_id=1, source_target_pairs={{0,1},{1,3},{3,2},{2,0},{4,5},{5,7},{7,6},{6,4},{8,9},{9,11},{11,1... | collective-permute-start | bytes 405512 | tf_op jit(solution)/shard_map/ppermute | solution.py:42
  29.9 3.8 %own.1 = (f32[4,256,512]{2,1,0:T(8,128)}, f32[2,256,512]{2,1,0:T(8,128)S(1)}) custom-call(bf16[1024,512]{1,0:T(8,128)(2,1)S(1)} %get-tuple-element.18.s_hi, bf16[1024,512]{1,0:T(8,128)(2,1)S(1)} %get-tuple-element.19.s_lo, f32[2,8,4224]{2,1,0:T(8,128)S(1)} %get-tuple-element.20.refs_0_, f32[2,8,4224]{2,1,0:T(8,128)S(1)} %collective-permute-done.refs_1_, ...), custom_call_target="tpu_custom_call" | custom-call | flops 1610612736 | bytes 5242880 | tf_op jit(solution)/shard_map/own/pallas_call | solution.py:361
  33.6 0.1 collective-permute-done.13.refs_3_
  33.7 1.4 %collective-permute-done.12.refs_2_ = f32[8,4224]{1,0:T(8,128)S(1)} collective-permute-done((f32[8,4224]{1,0:T(8,128)S(1)}, f32[8,4224]{1,0:T(8,128)S(1)}, u32[]{:S(2)}, u32[]{:S(2)}) %collective-permute-start.12) | collective-permute-done | bytes 135200 | tf_op jit(solution)/shard_map/ppermute | solution.py:42
  35.1 0.9 %collective-permute-done.11.refs_1_ = f32[8,4224]{1,0:T(8,128)S(1)} collective-permute-done((f32[8,4224]{1,0:T(8,128)S(1)}, f32[8,4224]{1,0:T(8,128)S(1)}, u32[]{:S(2)}, u32[]{:S(2)}) %collective-permute-start.11) | collective-permute-done | bytes 135200 | tf_op jit(solution)/shard_map/ppermute | solution.py:42
  36.0 1.7 %halo.1 = f32[4,256,512]{2,1,0:T(8,128)} custom-call(f32[4,256,512]{2,1,0:T(8,128)} %get-tuple-element.21.total_hbm, f32[2,256,512]{2,1,0:T(8,128)S(1)} %get-tuple-element.22.edge_ref, bf16[1024,512]{1,0:T(8,128)(2,1)S(1)} %get-tuple-element.18.s_hi, bf16[1024,512]{1,0:T(8,128)(2,1)S(1)} %get-tuple-element.19.s_lo, ...), custom_call_target="tpu_custom_call", output_to_operand_aliasing={{}: (0, {})} | custom-call | tf_op jit(solution)/shard_map/halo/pallas_call | solution.py:375
  (12 shorter events, 0.1 us)
Async XLA Ops:
  1.1 9.5 %collective-permute-start.1 = (f32[2,8,4224]{2,1,0:T(8,128)S(1)}, f32[2,8,4224]{2,1,0:T(8,128)S(1)}, u32[]{:S(2)}, u32[]{:S(2)}) collective-permute-start(f32[2,8,4224]{2,1,0:T(8,128)S(1)} %get-tuple-element.20.refs_0_), channel_id=1, source_target_pairs={{0,2},{1,0},{3,1},{2,3},{4,6},{5,4},{7,5},{6,7},{8,10},{9,8},{11,9... | collective-permute-start | bytes 811016 | tf_op jit(solution)/shard_map/ppermute | solution.py:42
  4.1 9.3 %collective-permute-start = (f32[2,8,4224]{2,1,0:T(8,128)S(1)}, f32[2,8,4224]{2,1,0:T(8,128)S(1)}, u32[]{:S(2)}, u32[]{:S(2)}) collective-permute-start(f32[2,8,4224]{2,1,0:T(8,128)S(1)} %get-tuple-element.20.refs_0_), channel_id=1, source_target_pairs={{0,1},{1,3},{3,2},{2,0},{4,5},{5,7},{7,6},{6,4},{8,9},{9,11},{11,1... | collective-permute-start | bytes 811016 | tf_op jit(solution)/shard_map/ppermute | solution.py:42
  4.2 16.4 %collective-permute-start.5 = (f32[8,2176]{1,0:T(8,128)S(1)}, f32[8,2176]{1,0:T(8,128)S(1)}, u32[]{:S(2)}, u32[]{:S(2)}) collective-permute-start(f32[8,2176]{1,0:T(8,128)S(1)} %get-tuple-element.25), channel_id=1, source_target_pairs={{0,4},{4,0},{8,12},{12,8},{16,20},{20,16},{24,28},{28,24},{1,5},{5... | collective-permute-start | bytes 208904 | tf_op jit(solution)/shard_map/ppermute | solution.py:42
  4.2 16.5 %collective-permute-start.6 = (f32[8,2176]{1,0:T(8,128)S(1)}, f32[8,2176]{1,0:T(8,128)S(1)}, u32[]{:S(2)}, u32[]{:S(2)}) collective-permute-start(f32[8,2176]{1,0:T(8,128)S(1)} %get-tuple-element.26), channel_id=1, source_target_pairs={{0,8},{4,12},{8,0},{12,4},{16,24},{20,28},{24,16},{28,20},{1,9},{5... | collective-permute-start | bytes 208904 | tf_op jit(solution)/shard_map/ppermute | solution.py:42
  6.2 15.2 %collective-permute-start.7 = (f32[8,2176]{1,0:T(8,128)S(1)}, f32[8,2176]{1,0:T(8,128)S(1)}, u32[]{:S(2)}, u32[]{:S(2)}) collective-permute-start(f32[8,2176]{1,0:T(8,128)S(1)} %get-tuple-element.27), channel_id=1, source_target_pairs={{0,12},{4,8},{8,4},{12,0},{16,28},{20,24},{24,20},{28,16},{1,13},{... | collective-permute-start | bytes 208904 | tf_op jit(solution)/shard_map/ppermute | solution.py:42
  10.6 8.5 %collective-permute-start.4 = (f32[8,4224]{1,0:T(8,128)S(1)}, f32[8,4224]{1,0:T(8,128)S(1)}, u32[]{:S(2)}, u32[]{:S(2)}) collective-permute-start(f32[8,4224]{1,0:T(8,128)S(1)} %get-tuple-element.24), channel_id=1, source_target_pairs={{0,16},{4,20},{8,24},{12,28},{16,0},{20,4},{24,8},{28,12},{1,17},{... | collective-permute-start | bytes 405512 | tf_op jit(solution)/shard_map/ppermute | solution.py:42
  13.4 16.4 %collective-permute-start.3 = (f32[8,4224]{1,0:T(8,128)S(1)}, f32[8,4224]{1,0:T(8,128)S(1)}, u32[]{:S(2)}, u32[]{:S(2)}) collective-permute-start(f32[8,4224]{1,0:T(8,128)S(1)} %slice_bitcast_fusion), channel_id=1, source_target_pairs={{0,2},{1,0},{3,1},{2,3},{4,6},{5,4},{7,5},{6,7},{8,10},{9,8},{11,9... | collective-permute-start | bytes 405512 | tf_op jit(solution)/shard_map/ppermute | solution.py:42
  19.1 10.7 %collective-permute-start.2 = (f32[8,4224]{1,0:T(8,128)S(1)}, f32[8,4224]{1,0:T(8,128)S(1)}, u32[]{:S(2)}, u32[]{:S(2)}) collective-permute-start(f32[8,4224]{1,0:T(8,128)S(1)} %slice_bitcast_fusion.1), channel_id=1, source_target_pairs={{0,1},{1,3},{3,2},{2,0},{4,5},{5,7},{7,6},{6,4},{8,9},{9,11},{11,1... | collective-permute-start | bytes 405512 | tf_op jit(solution)/shard_map/ppermute | solution.py:42
  20.6 3.6 %collective-permute-start.8 = (f32[8,2176]{1,0:T(8,128)S(1)}, f32[8,2176]{1,0:T(8,128)S(1)}, u32[]{:S(2)}, u32[]{:S(2)}) collective-permute-start(f32[8,2176]{1,0:T(8,128)S(1)} %get-tuple-element.28), channel_id=1, source_target_pairs={{0,4},{4,0},{8,12},{12,8},{16,20},{20,16},{24,28},{28,24},{1,5},{5... | collective-permute-start | bytes 208904 | tf_op jit(solution)/shard_map/ppermute | solution.py:42
  20.7 5.1 %collective-permute-start.9 = (f32[8,2176]{1,0:T(8,128)S(1)}, f32[8,2176]{1,0:T(8,128)S(1)}, u32[]{:S(2)}, u32[]{:S(2)}) collective-permute-start(f32[8,2176]{1,0:T(8,128)S(1)} %get-tuple-element.29), channel_id=1, source_target_pairs={{0,8},{4,12},{8,0},{12,4},{16,24},{20,28},{24,16},{28,20},{1,9},{5... | collective-permute-start | bytes 208904 | tf_op jit(solution)/shard_map/ppermute | solution.py:42
  21.4 4.8 %collective-permute-start.10 = (f32[8,2176]{1,0:T(8,128)S(1)}, f32[8,2176]{1,0:T(8,128)S(1)}, u32[]{:S(2)}, u32[]{:S(2)}) collective-permute-start(f32[8,2176]{1,0:T(8,128)S(1)} %get-tuple-element.30), channel_id=1, source_target_pairs={{0,12},{4,8},{8,4},{12,0},{16,28},{20,24},{24,20},{28,16},{1,13},{... | collective-permute-start | bytes 208904 | tf_op jit(solution)/shard_map/ppermute | solution.py:42
  26.3 7.4 %collective-permute-start.13 = (f32[8,4224]{1,0:T(8,128)S(1)}, f32[8,4224]{1,0:T(8,128)S(1)}, u32[]{:S(2)}, u32[]{:S(2)}) collective-permute-start(f32[8,4224]{1,0:T(8,128)S(1)} %pick.1.refs_0_), channel_id=1, source_target_pairs={{0,3},{1,2},{2,1},{3,0},{4,7},{5,6},{6,5},{7,4},{8,11},{9,10},{10,... | collective-permute-start | bytes 405512 | tf_op jit(solution)/shard_map/ppermute | solution.py:42
  27.8 7.3 %collective-permute-start.12 = (f32[8,4224]{1,0:T(8,128)S(1)}, f32[8,4224]{1,0:T(8,128)S(1)}, u32[]{:S(2)}, u32[]{:S(2)}) collective-permute-start(f32[8,4224]{1,0:T(8,128)S(1)} %pick.1.refs_0_), channel_id=1, source_target_pairs={{0,2},{1,0},{3,1},{2,3},{4,6},{5,4},{7,5},{6,7},{8,10},{9,8},{11,9... | collective-permute-start | bytes 405512 | tf_op jit(solution)/shard_map/ppermute | solution.py:42
  29.3 6.7 %collective-permute-start.11 = (f32[8,4224]{1,0:T(8,128)S(1)}, f32[8,4224]{1,0:T(8,128)S(1)}, u32[]{:S(2)}, u32[]{:S(2)}) collective-permute-start(f32[8,4224]{1,0:T(8,128)S(1)} %pick.1.refs_0_), channel_id=1, source_target_pairs={{0,1},{1,3},{3,2},{2,0},{4,5},{5,7},{7,6},{6,4},{8,9},{9,11},{11,1... | collective-permute-start | bytes 405512 | tf_op jit(solution)/shard_map/ppermute | solution.py:42

commit v2 on v1

--- a/solution.py
+++ b/solution.py
@@ -191,13 +191,6 @@
             halo_ref[:, 2 * at :] = jnp.where(upper, values[1], values[0])
 
 
-def joined(left, right, dims):
-    axis = dims[1][0]
-    lefts = jnp.concatenate([left[0], left[0], left[1]], axis=1)
-    rights = jnp.concatenate([right[0], right[1], right[0]], axis=axis)
-    return lax.dot_general(lefts, rights, (dims, ((), ())), preferred_element_type=jnp.float32)
-
-
 def prep_kernel(state_hbm, hi_ref, lo_ref, state_ref, sems):
     levels, rows = state_ref.shape[:2]
     loads = [pltpu.make_async_copy(state_hbm.at[l], state_ref.at[l], sems.at[l]) for l in range(levels)]
@@ -259,28 +252,30 @@
     for s, shift in enumerate((-SECT_W, SECT_W)):
         at = 2 * s * wide
         anom = split(jnp.concatenate([unfolded(h[:, at : at + wide], members) for h in halo_refs], axis=0))
-        both = jnp.concatenate(anom, axis=0)
+        both = jnp.concatenate([anom[0], anom[0], anom[1], anom[1]], axis=0)
         high, low = (
             jnp.concatenate([ref[l * columns + starts[s] : l * columns + starts[s] + EDGE, :] for l in range(levels)], axis=0)
             for ref in (s_hi, s_lo)
         )
         wide_dot = dot(high, both)
-        covar = wide_dot[:, :count] + (wide_dot[:, count:] + dot(low, anom[0]))
+        covar = wide_dot[:, : 2 * count] + (wide_dot[:, 2 * count :] + dot(low, both[: 2 * count]))
         row = s * (SUB // 2)
-        tiles = [h[row : row + 1, 4 * wide :] for h in halo_refs]
+        tiles = [h[row : row + 1, 4 * wide :] for h in halo_refs] * 2
         groups = []
-        for g in range(0, blocks, per):
+        for g in range(0, 2 * blocks, per):
             cells = tiles[g]
-            for b in range(1, min(per, blocks - g)):
+            for b in range(1, min(per, 2 * blocks - g)):
                 cells = jnp.where(lane >= b * CAP, tiles[g + b], cells)
             groups.append(cells)
-        cells = jnp.concatenate(groups, axis=1)[:, :count]
+        cells = jnp.concatenate(groups, axis=1)[:, : 2 * count]
         rho = taper(starts[s], EDGE, cells, shift) / (members - 1)
         covars.append(split((covar.reshape(levels, EDGE, -1) * rho[None]).reshape(levels * EDGE, -1)))
         weights.append(split(jnp.concatenate([unfolded(h[:, at + wide : at + 2 * wide], members) for h in halo_refs], axis=0)))
     stores = []
     for s in range(2):
-        out_ref[s] = edge_ref[s] + joined(covars[s], weights[s], NN)
+        lefts = jnp.concatenate(covars[s], axis=1)
+        rights = jnp.concatenate(weights[s] * 2, axis=0)
+        out_ref[s] = edge_ref[s] + lax.dot_general(lefts, rights, (NN, ((), ())), preferred_element_type=jnp.float32)
         for l in range(levels):
             store = pltpu.make_async_copy(
                 out_ref.at[s, pl.ds(l * EDGE, EDGE)], out_hbm.at[l, pl.ds(starts[s], EDGE)], out_sem.at[s, l]

time: 37.9 us -> 37.7 us (level)
  transfers between devices with their start and end apart: 14 -> 14, of which waited for: 7 -> 7; matrix products, arithmetic and copies ran while one was open for 0% -> 0% of each run, Pallas kernels for 14% -> 15%
where the time goes in v2:
time: 37.7 us; the launch traced here: 37.6 us
  starting transfers between devices  16.6 us (44%)
  waiting for transfers between devices  12.8 us (34%)
  Pallas kernels  8.09 us (21%)
    ppermute x14, starting transfers between devices, exchange(): return lax.ppermute(value, axis, pairs)  16.6 us
    ppermute x14, waiting for transfers between devices, exchange(): return lax.ppermute(value, axis, pairs)  12.8 us
    pallas_call x1, Pallas kernels, on_device(): pl.pallas_call(functools.partial(own_kernel, tree), out_shape=[jax.ShapeD...  3.75 us
    pallas_call x1, Pallas kernels, on_device(): pl.pallas_call(prep_kernel, out_shape=[jax.ShapeDtypeStruct(halves, bf16)...  1.64 us
    pallas_call x1, Pallas kernels, on_device(): pl.pallas_call(functools.partial(halo_kernel, blocks), out_shape=jax.Shap...  1.57 us
    pallas_call x1, Pallas kernels, on_device(): pl.pallas_call(pack_kernel, out_shape=[jax.ShapeDtypeStruct((2, SUB, coun...  1.06 us
  transfers between devices with their start and end apart: 14, of which 7 were waited for; matrix products, arithmetic and copies ran while one was open for 0% of the time, Pallas kernels for 15%

profile of v2, /device:TPU:0, one launch (start us, length us, event | category | flops | bytes accessed | tf_op | source)
XLA Modules:
  0.0 37.6 jit_solution(10299524981347773960)
XLA Ops:
  0.0 1.1 %pack.1 = (f32[2,8,4224]{2,1,0:T(8,128)S(1)}, s32[5,8,128]{2,1,0:T(8,128)S(1)}, f32[8,4224]{1,0:T(8,128)S(1)}, f32[8,2176]{1,0:T(8,128)S(1)}, f32[8,2176]{1,0:T(8,128)S(1)}, /*index=5*/f32[8,2176]{1,0:T(8,128)S(1)}) custom-call(s32[8]{0:T(128)} %sector_hbm.1, f32[1,64,512]{2,1,0:T(8,128)} %anom_hbm.1, f32[1,64,512]{2,1,0:T(8,128)} %weight_hbm.1, ...), custom_call_target="tpu_custom_call" | custom-call | tf_op jit(solution)/shard_map/pack/pallas_call | solution.py:301
  1.1 3.0 %collective-permute-start.1 = (f32[2,8,4224]{2,1,0:T(8,128)S(1)}, f32[2,8,4224]{2,1,0:T(8,128)S(1)}, u32[]{:S(2)}, u32[]{:S(2)}) collective-permute-start(f32[2,8,4224]{2,1,0:T(8,128)S(1)} %get-tuple-element.20.refs_0_), channel_id=1, source_target_pairs={{0,2},{1,0},{3,1},{2,3},{4,6},{5,4},{7,5},{6,7},{8,10},{9,8},{11,9... | collective-permute-start | bytes 811016 | tf_op jit(solution)/shard_map/ppermute | solution.py:42
  4.1 0.0 collective-permute-start
  4.2 2.0 %collective-permute-start.6 = (f32[8,2176]{1,0:T(8,128)S(1)}, f32[8,2176]{1,0:T(8,128)S(1)}, u32[]{:S(2)}, u32[]{:S(2)}) collective-permute-start(f32[8,2176]{1,0:T(8,128)S(1)} %get-tuple-element.26), channel_id=1, source_target_pairs={{0,8},{4,12},{8,0},{12,4},{16,24},{20,28},{24,16},{28,20},{1,9},{5... | collective-permute-start | bytes 208904 | tf_op jit(solution)/shard_map/ppermute | solution.py:42
  6.2 0.1 collective-permute-start.7
  6.3 4.3 %collective-permute-done.1.refs_2_ = f32[2,8,4224]{2,1,0:T(8,128)S(1)} collective-permute-done((f32[2,8,4224]{2,1,0:T(8,128)S(1)}, f32[2,8,4224]{2,1,0:T(8,128)S(1)}, u32[]{:S(2)}, u32[]{:S(2)}) %collective-permute-start.1) | collective-permute-done | bytes 270368 | tf_op jit(solution)/shard_map/ppermute | solution.py:42
  10.6 2.8 %collective-permute-start.4 = (f32[8,4224]{1,0:T(8,128)S(1)}, f32[8,4224]{1,0:T(8,128)S(1)}, u32[]{:S(2)}, u32[]{:S(2)}) collective-permute-start(f32[8,4224]{1,0:T(8,128)S(1)} %get-tuple-element.24), channel_id=1, source_target_pairs={{0,16},{4,20},{8,24},{12,28},{16,0},{20,4},{24,8},{28,12},{1,17},{... | collective-permute-start | bytes 405512 | tf_op jit(solution)/shard_map/ppermute | solution.py:42
  13.4 1.6 %collective-permute-start.3 = (f32[8,4224]{1,0:T(8,128)S(1)}, f32[8,4224]{1,0:T(8,128)S(1)}, u32[]{:S(2)}, u32[]{:S(2)}) collective-permute-start(f32[8,4224]{1,0:T(8,128)S(1)} %slice_bitcast_fusion), channel_id=1, source_target_pairs={{0,2},{1,0},{3,1},{2,3},{4,6},{5,4},{7,5},{6,7},{8,10},{9,8},{11,9... | collective-permute-start | bytes 405512 | tf_op jit(solution)/shard_map/ppermute | solution.py:42
  15.0 4.1 %collective-permute-done.4.cross_ref = f32[8,4224]{1,0:T(8,128)S(1)} collective-permute-done((f32[8,4224]{1,0:T(8,128)S(1)}, f32[8,4224]{1,0:T(8,128)S(1)}, u32[]{:S(2)}, u32[]{:S(2)}) %collective-permute-start.4) | collective-permute-done | bytes 135200 | tf_op jit(solution)/shard_map/ppermute | solution.py:42
  19.1 1.5 %collective-permute-start.2 = (f32[8,4224]{1,0:T(8,128)S(1)}, f32[8,4224]{1,0:T(8,128)S(1)}, u32[]{:S(2)}, u32[]{:S(2)}) collective-permute-start(f32[8,4224]{1,0:T(8,128)S(1)} %slice_bitcast_fusion.1), channel_id=1, source_target_pairs={{0,1},{1,3},{3,2},{2,0},{4,5},{5,7},{7,6},{6,4},{8,9},{9,11},{11,1... | collective-permute-start | bytes 405512 | tf_op jit(solution)/shard_map/ppermute | solution.py:42
  20.6 0.1 collective-permute-start.8
  20.7 0.7 %collective-permute-start.9 = (f32[8,2176]{1,0:T(8,128)S(1)}, f32[8,2176]{1,0:T(8,128)S(1)}, u32[]{:S(2)}, u32[]{:S(2)}) collective-permute-start(f32[8,2176]{1,0:T(8,128)S(1)} %get-tuple-element.29), channel_id=1, source_target_pairs={{0,8},{4,12},{8,0},{12,4},{16,24},{20,28},{24,16},{28,20},{1,9},{5... | collective-permute-start | bytes 208904 | tf_op jit(solution)/shard_map/ppermute | solution.py:42
  21.4 1.1 %collective-permute-start.10 = (f32[8,2176]{1,0:T(8,128)S(1)}, f32[8,2176]{1,0:T(8,128)S(1)}, u32[]{:S(2)}, u32[]{:S(2)}) collective-permute-start(f32[8,2176]{1,0:T(8,128)S(1)} %get-tuple-element.30), channel_id=1, source_target_pairs={{0,12},{4,8},{8,4},{12,0},{16,28},{20,24},{24,20},{28,16},{1,13},{... | collective-permute-start | bytes 208904 | tf_op jit(solution)/shard_map/ppermute | solution.py:42
  22.5 1.6 %prep.1 = (bf16[1024,512]{1,0:T(8,128)(2,1)S(1)}, bf16[1024,512]{1,0:T(8,128)(2,1)S(1)}) custom-call(f32[4,256,512]{2,1,0:T(8,128)} %bitcast.6), custom_call_target="tpu_custom_call" | custom-call | tf_op jit(solution)/shard_map/prep/pallas_call | solution.py:346
  24.2 1.6 %collective-permute-done.9.refs_4_ = f32[8,2176]{1,0:T(8,128)S(1)} collective-permute-done((f32[8,2176]{1,0:T(8,128)S(1)}, f32[8,2176]{1,0:T(8,128)S(1)}, u32[]{:S(2)}, u32[]{:S(2)}) %collective-permute-start.9) | collective-permute-done | bytes 69664 | tf_op jit(solution)/shard_map/ppermute | solution.py:42
  25.8 0.4 %collective-permute-done.10.refs_5_ = f32[8,2176]{1,0:T(8,128)S(1)} collective-permute-done((f32[8,2176]{1,0:T(8,128)S(1)}, f32[8,2176]{1,0:T(8,128)S(1)}, u32[]{:S(2)}, u32[]{:S(2)}) %collective-permute-start.10) | collective-permute-done | bytes 69664 | tf_op jit(solution)/shard_map/ppermute | solution.py:42
  26.3 1.6 %collective-permute-start.13 = (f32[8,4224]{1,0:T(8,128)S(1)}, f32[8,4224]{1,0:T(8,128)S(1)}, u32[]{:S(2)}, u32[]{:S(2)}) collective-permute-start(f32[8,4224]{1,0:T(8,128)S(1)} %pick.1.refs_0_), channel_id=1, source_target_pairs={{0,3},{1,2},{2,1},{3,0},{4,7},{5,6},{6,5},{7,4},{8,11},{9,10},{10,... | collective-permute-start | bytes 405512 | tf_op jit(solution)/shard_map/ppermute | solution.py:42
  27.8 1.5 %collective-permute-start.12 = (f32[8,4224]{1,0:T(8,128)S(1)}, f32[8,4224]{1,0:T(8,128)S(1)}, u32[]{:S(2)}, u32[]{:S(2)}) collective-permute-start(f32[8,4224]{1,0:T(8,128)S(1)} %pick.1.refs_0_), channel_id=1, source_target_pairs={{0,2},{1,0},{3,1},{2,3},{4,6},{5,4},{7,5},{6,7},{8,10},{9,8},{11,9... | collective-permute-start | bytes 405512 | tf_op jit(solution)/shard_map/ppermute | solution.py:42
  29.3 0.5 %collective-permute-start.11 = (f32[8,4224]{1,0:T(8,128)S(1)}, f32[8,4224]{1,0:T(8,128)S(1)}, u32[]{:S(2)}, u32[]{:S(2)}) collective-permute-start(f32[8,4224]{1,0:T(8,128)S(1)} %pick.1.refs_0_), channel_id=1, source_target_pairs={{0,1},{1,3},{3,2},{2,0},{4,5},{5,7},{7,6},{6,4},{8,9},{9,11},{11,1... | collective-permute-start | bytes 405512 | tf_op jit(solution)/shard_map/ppermute | solution.py:42
  29.9 3.8 %own.1 = (f32[4,256,512]{2,1,0:T(8,128)}, f32[2,256,512]{2,1,0:T(8,128)S(1)}) custom-call(bf16[1024,512]{1,0:T(8,128)(2,1)S(1)} %get-tuple-element.18.s_hi, bf16[1024,512]{1,0:T(8,128)(2,1)S(1)} %get-tuple-element.19.s_lo, f32[2,8,4224]{2,1,0:T(8,128)S(1)} %get-tuple-element.20.refs_0_, f32[2,8,4224]{2,1,0:T(8,128)S(1)} %collective-permute-done.refs_1_, ...), custom_call_target="tpu_custom_call" | custom-call | flops 1610612736 | bytes 5242880 | tf_op jit(solution)/shard_map/own/pallas_call | solution.py:356
  33.6 0.1 collective-permute-done.13.refs_3_
  33.7 1.4 %collective-permute-done.12.refs_2_ = f32[8,4224]{1,0:T(8,128)S(1)} collective-permute-done((f32[8,4224]{1,0:T(8,128)S(1)}, f32[8,4224]{1,0:T(8,128)S(1)}, u32[]{:S(2)}, u32[]{:S(2)}) %collective-permute-start.12) | collective-permute-done | bytes 135200 | tf_op jit(solution)/shard_map/ppermute | solution.py:42
  35.1 0.9 %collective-permute-done.11.refs_1_ = f32[8,4224]{1,0:T(8,128)S(1)} collective-permute-done((f32[8,4224]{1,0:T(8,128)S(1)}, f32[8,4224]{1,0:T(8,128)S(1)}, u32[]{:S(2)}, u32[]{:S(2)}) %collective-permute-start.11) | collective-permute-done | bytes 135200 | tf_op jit(solution)/shard_map/ppermute | solution.py:42
  36.0 1.6 %halo.1 = f32[4,256,512]{2,1,0:T(8,128)} custom-call(f32[4,256,512]{2,1,0:T(8,128)} %get-tuple-element.21.total_hbm, f32[2,256,512]{2,1,0:T(8,128)S(1)} %get-tuple-element.22.edge_ref, bf16[1024,512]{1,0:T(8,128)(2,1)S(1)} %get-tuple-element.18.s_hi, bf16[1024,512]{1,0:T(8,128)(2,1)S(1)} %get-tuple-element.19.s_lo, ...), custom_call_target="tpu_custom_call", output_to_operand_aliasing={{}: (0, {})} | custom-call | tf_op jit(solution)/shard_map/halo/pallas_call | solution.py:370
  (12 shorter events, 0.1 us)
Async XLA Ops:
  1.1 9.5 %collective-permute-start.1 = (f32[2,8,4224]{2,1,0:T(8,128)S(1)}, f32[2,8,4224]{2,1,0:T(8,128)S(1)}, u32[]{:S(2)}, u32[]{:S(2)}) collective-permute-start(f32[2,8,4224]{2,1,0:T(8,128)S(1)} %get-tuple-element.20.refs_0_), channel_id=1, source_target_pairs={{0,2},{1,0},{3,1},{2,3},{4,6},{5,4},{7,5},{6,7},{8,10},{9,8},{11,9... | collective-permute-start | bytes 811016 | tf_op jit(solution)/shard_map/ppermute | solution.py:42
  4.1 9.3 %collective-permute-start = (f32[2,8,4224]{2,1,0:T(8,128)S(1)}, f32[2,8,4224]{2,1,0:T(8,128)S(1)}, u32[]{:S(2)}, u32[]{:S(2)}) collective-permute-start(f32[2,8,4224]{2,1,0:T(8,128)S(1)} %get-tuple-element.20.refs_0_), channel_id=1, source_target_pairs={{0,1},{1,3},{3,2},{2,0},{4,5},{5,7},{7,6},{6,4},{8,9},{9,11},{11,1... | collective-permute-start | bytes 811016 | tf_op jit(solution)/shard_map/ppermute | solution.py:42
  4.2 16.4 %collective-permute-start.5 = (f32[8,2176]{1,0:T(8,128)S(1)}, f32[8,2176]{1,0:T(8,128)S(1)}, u32[]{:S(2)}, u32[]{:S(2)}) collective-permute-start(f32[8,2176]{1,0:T(8,128)S(1)} %get-tuple-element.25), channel_id=1, source_target_pairs={{0,4},{4,0},{8,12},{12,8},{16,20},{20,16},{24,28},{28,24},{1,5},{5... | collective-permute-start | bytes 208904 | tf_op jit(solution)/shard_map/ppermute | solution.py:42
  4.2 16.5 %collective-permute-start.6 = (f32[8,2176]{1,0:T(8,128)S(1)}, f32[8,2176]{1,0:T(8,128)S(1)}, u32[]{:S(2)}, u32[]{:S(2)}) collective-permute-start(f32[8,2176]{1,0:T(8,128)S(1)} %get-tuple-element.26), channel_id=1, source_target_pairs={{0,8},{4,12},{8,0},{12,4},{16,24},{20,28},{24,16},{28,20},{1,9},{5... | collective-permute-start | bytes 208904 | tf_op jit(solution)/shard_map/ppermute | solution.py:42
  6.2 15.2 %collective-permute-start.7 = (f32[8,2176]{1,0:T(8,128)S(1)}, f32[8,2176]{1,0:T(8,128)S(1)}, u32[]{:S(2)}, u32[]{:S(2)}) collective-permute-start(f32[8,2176]{1,0:T(8,128)S(1)} %get-tuple-element.27), channel_id=1, source_target_pairs={{0,12},{4,8},{8,4},{12,0},{16,28},{20,24},{24,20},{28,16},{1,13},{... | collective-permute-start | bytes 208904 | tf_op jit(solution)/shard_map/ppermute | solution.py:42
  10.6 8.5 %collective-permute-start.4 = (f32[8,4224]{1,0:T(8,128)S(1)}, f32[8,4224]{1,0:T(8,128)S(1)}, u32[]{:S(2)}, u32[]{:S(2)}) collective-permute-start(f32[8,4224]{1,0:T(8,128)S(1)} %get-tuple-element.24), channel_id=1, source_target_pairs={{0,16},{4,20},{8,24},{12,28},{16,0},{20,4},{24,8},{28,12},{1,17},{... | collective-permute-start | bytes 405512 | tf_op jit(solution)/shard_map/ppermute | solution.py:42
  13.4 16.4 %collective-permute-start.3 = (f32[8,4224]{1,0:T(8,128)S(1)}, f32[8,4224]{1,0:T(8,128)S(1)}, u32[]{:S(2)}, u32[]{:S(2)}) collective-permute-start(f32[8,4224]{1,0:T(8,128)S(1)} %slice_bitcast_fusion), channel_id=1, source_target_pairs={{0,2},{1,0},{3,1},{2,3},{4,6},{5,4},{7,5},{6,7},{8,10},{9,8},{11,9... | collective-permute-start | bytes 405512 | tf_op jit(solution)/shard_map/ppermute | solution.py:42
  19.1 10.7 %collective-permute-start.2 = (f32[8,4224]{1,0:T(8,128)S(1)}, f32[8,4224]{1,0:T(8,128)S(1)}, u32[]{:S(2)}, u32[]{:S(2)}) collective-permute-start(f32[8,4224]{1,0:T(8,128)S(1)} %slice_bitcast_fusion.1), channel_id=1, source_target_pairs={{0,1},{1,3},{3,2},{2,0},{4,5},{5,7},{7,6},{6,4},{8,9},{9,11},{11,1... | collective-permute-start | bytes 405512 | tf_op jit(solution)/shard_map/ppermute | solution.py:42
  20.6 3.6 %collective-permute-start.8 = (f32[8,2176]{1,0:T(8,128)S(1)}, f32[8,2176]{1,0:T(8,128)S(1)}, u32[]{:S(2)}, u32[]{:S(2)}) collective-permute-start(f32[8,2176]{1,0:T(8,128)S(1)} %get-tuple-element.28), channel_id=1, source_target_pairs={{0,4},{4,0},{8,12},{12,8},{16,20},{20,16},{24,28},{28,24},{1,5},{5... | collective-permute-start | bytes 208904 | tf_op jit(solution)/shard_map/ppermute | solution.py:42
  20.7 5.1 %collective-permute-start.9 = (f32[8,2176]{1,0:T(8,128)S(1)}, f32[8,2176]{1,0:T(8,128)S(1)}, u32[]{:S(2)}, u32[]{:S(2)}) collective-permute-start(f32[8,2176]{1,0:T(8,128)S(1)} %get-tuple-element.29), channel_id=1, source_target_pairs={{0,8},{4,12},{8,0},{12,4},{16,24},{20,28},{24,16},{28,20},{1,9},{5... | collective-permute-start | bytes 208904 | tf_op jit(solution)/shard_map/ppermute | solution.py:42
  21.4 4.8 %collective-permute-start.10 = (f32[8,2176]{1,0:T(8,128)S(1)}, f32[8,2176]{1,0:T(8,128)S(1)}, u32[]{:S(2)}, u32[]{:S(2)}) collective-permute-start(f32[8,2176]{1,0:T(8,128)S(1)} %get-tuple-element.30), channel_id=1, source_target_pairs={{0,12},{4,8},{8,4},{12,0},{16,28},{20,24},{24,20},{28,16},{1,13},{... | collective-permute-start | bytes 208904 | tf_op jit(solution)/shard_map/ppermute | solution.py:42
  26.3 7.4 %collective-permute-start.13 = (f32[8,4224]{1,0:T(8,128)S(1)}, f32[8,4224]{1,0:T(8,128)S(1)}, u32[]{:S(2)}, u32[]{:S(2)}) collective-permute-start(f32[8,4224]{1,0:T(8,128)S(1)} %pick.1.refs_0_), channel_id=1, source_target_pairs={{0,3},{1,2},{2,1},{3,0},{4,7},{5,6},{6,5},{7,4},{8,11},{9,10},{10,... | collective-permute-start | bytes 405512 | tf_op jit(solution)/shard_map/ppermute | solution.py:42
  27.8 7.3 %collective-permute-start.12 = (f32[8,4224]{1,0:T(8,128)S(1)}, f32[8,4224]{1,0:T(8,128)S(1)}, u32[]{:S(2)}, u32[]{:S(2)}) collective-permute-start(f32[8,4224]{1,0:T(8,128)S(1)} %pick.1.refs_0_), channel_id=1, source_target_pairs={{0,2},{1,0},{3,1},{2,3},{4,6},{5,4},{7,5},{6,7},{8,10},{9,8},{11,9... | collective-permute-start | bytes 405512 | tf_op jit(solution)/shard_map/ppermute | solution.py:42
  29.3 6.7 %collective-permute-start.11 = (f32[8,4224]{1,0:T(8,128)S(1)}, f32[8,4224]{1,0:T(8,128)S(1)}, u32[]{:S(2)}, u32[]{:S(2)}) collective-permute-start(f32[8,4224]{1,0:T(8,128)S(1)} %pick.1.refs_0_), channel_id=1, source_target_pairs={{0,1},{1,3},{3,2},{2,0},{4,5},{5,7},{7,6},{6,4},{8,9},{9,11},{11,1... | collective-permute-start | bytes 405512 | tf_op jit(solution)/shard_map/ppermute | solution.py:42
